TPU v7x, 32 devices: a whole 2x2x4 slice. The times are simulated.
32 devices in a mesh: pipe: 8 (over z, y), head: 4 (over x, core).
Axes of the slice: x: 2, y: 2, z: 4, core: 2. Of those that a mesh axis runs over, the one named last changes fastest.
Arguments:
- queries: bfloat16 [2, 2048, 8192], P(None, 'pipe', 'head'), may hold values from -150 to 150
- keys: bfloat16 [2048, 1024], P(('pipe', 'head')), may hold values from -7 to 7
- values: bfloat16 [2048, 1024], P(('pipe', 'head')), may hold values from -6 to 6
- slice_index: int32 [2, 8], replicated, may hold values from 0 to 7, each once within a row
Outputs:
- attended: bfloat16 [2, 2048, 8192], P(None, 'pipe', 'head')
Inputs may be any that keep to these rules, and one draw needn't show every extreme that they name: Each row of slice_index is a permutation of 0 to 7.
All inputs are finite; a program needn't handle non-finite values.
Results may differ from a plain program's by a relative error of at most 0.0041.
Values may be sent and summed in bfloat16 or wider, within the bound.
A program may use at most 128 MiB of HBM per device.

v0:
```python
import math

import jax
import jax.numpy as jnp
from jax import lax
from jax.sharding import PartitionSpec as P

HEAD_SIZE = 128


NEG = -1e30


def blank_state(length, heads, query_group):
    return (
        jnp.full((length, heads, query_group), NEG, jnp.float32),
        jnp.zeros((length, heads, query_group), jnp.float32),
        jnp.zeros((length, heads, query_group, HEAD_SIZE), jnp.float32),
    )


def absorb(state, query, query_pos, key_block, value_block, key_start):
    best, total, accum = state
    scores = jnp.einsum(
        "rhgd,khd->rhgk", query, key_block, preferred_element_type=jnp.float32
    ) * HEAD_SIZE ** (-0.5)
    key_pos = key_start + jnp.arange(key_block.shape[0], dtype=jnp.int32)
    allowed = (key_pos[None, :] <= query_pos[:, None])[:, None, None, :]
    peak = jnp.maximum(best, jnp.max(jnp.where(allowed, scores, NEG), axis=-1))
    weights = jnp.where(allowed, jnp.exp(scores - peak[..., None]), 0.0)
    factor = jnp.exp(best - peak)
    total = total * factor + jnp.sum(weights, axis=-1)
    accum = accum * factor[..., None] + jnp.einsum(
        "rhgk,khd->rhgd",
        weights.astype(jnp.bfloat16),
        value_block,
        preferred_element_type=jnp.float32,
    )
    return (peak, total, accum)


def finish(state):
    best, total, accum = state
    result = (accum / total[..., None]).astype(jnp.bfloat16)
    return result.reshape(result.shape[0], -1)


def on_device(queries, keys, values, slice_index):
    key_cols, value_cols = (
        lax.all_to_all(keys, "head", split_axis=1, concat_axis=0, tiled=True),
        lax.all_to_all(values, "head", split_axis=1, concat_axis=0, tiled=True),
    )
    ticks, length, columns = queries.shape
    heads = key_cols.shape[1] // HEAD_SIZE
    query_group = columns // HEAD_SIZE // heads
    section_index = lax.axis_index("pipe")
    shaped = queries.reshape(ticks, length, heads, query_group, HEAD_SIZE)
    offsets = lax.dynamic_index_in_dim(slice_index, section_index, axis=1, keepdims=False) * length
    positions = offsets[:, None] + jnp.arange(length, dtype=jnp.int32)[None, :]
    initial = tuple((blank_state(length, heads, query_group) for tick_index in range(ticks)))
    key_piece = lax.all_gather(key_cols, "pipe", axis=0, tiled=True)
    value_piece = lax.all_gather(value_cols, "pipe", axis=0, tiled=True)
    extent = key_piece.shape[0]
    stride = extent if extent <= 2048 else math.gcd(extent, 2048)
    key_piece = key_piece.reshape(extent, heads, HEAD_SIZE)
    value_piece = value_piece.reshape(extent, heads, HEAD_SIZE)
    results = []
    for tick_index in range(ticks):

        def one_block(index, current, tick_index=tick_index):
            offset = index * stride
            key_start = offset

            def compute(carried):
                key_block = lax.dynamic_slice_in_dim(key_piece, offset, stride, 0)
                value_block = lax.dynamic_slice_in_dim(value_piece, offset, stride, 0)
                return absorb(
                    carried,
                    shaped[tick_index],
                    positions[tick_index],
                    key_block,
                    value_block,
                    key_start,
                )

            return lax.cond(
                key_start <= positions[tick_index, length - 1],
                compute,
                lambda carried: carried,
                current,
            )

        results.append(lax.fori_loop(0, extent // stride, one_block, initial[tick_index]))
    states = tuple(results)
    return jnp.stack([finish(state) for state in states])


def solution(mesh):
    return jax.shard_map(
        on_device,
        mesh=mesh,
        in_specs=(
            P(None, "pipe", "head"),
            P(("pipe", "head"), None),
            P(("pipe", "head"), None),
            P(),
        ),
        out_specs=P(None, "pipe", "head"),
        check_vma=False,
    )
```

profile of v0, /device:TPU:0, one launch (start us, length us, event | category | flops | bytes accessed | tf_op | source)
XLA Modules:
  0.0 214.6 jit_solution(6625736233731818834)
XLA Ops:
  6.5 0.0 all-gather.3.cloned.1.call-start
  6.5 0.9 copy.71
  7.5 8.7 %all_to_all.38 = bf16[64,4,256]{2,0,1:T(8,128)(2,1)} all-to-all(bf16[64,4,256]{2,0,1:T(8,128)(2,1)S(1)} %bitcast.103), channel_id=1, replica_groups=mesh['pipe'=8,'head'=4] {'head'}, dimensions={1} | all-to-all | bytes 262144 | tf_op jit(solution)/shard_map/all_to_all | solution.py:50
  16.2 0.0 all-gather.3.cloned.1.call-update
  16.2 0.0 all-gather.5.cloned.1.call-start
  16.3 0.9 copy.70
  17.2 7.6 %all_to_all.39 = bf16[64,4,256]{2,0,1:T(8,128)(2,1)} all-to-all(bf16[64,4,256]{2,0,1:T(8,128)(2,1)S(1)} %bitcast.104), channel_id=1, replica_groups=mesh['pipe'=8,'head'=4] {'head'}, dimensions={1} | all-to-all | bytes 262144 | tf_op jit(solution)/shard_map/all_to_all | solution.py:51
  24.8 0.0 all-gather.5.cloned.1.call-update
  24.9 0.9 multiply_reduce_fusion
  25.7 0.1 iota_add_fusion
  25.8 0.7 fusion.30
  27.1 2.9 %copy.39 = bf16[2,256,2048]{1,2,0:T(8,128)(2,1)S(1)} copy(bf16[2,256,2048]{2,1,0:T(8,128)(2,1)} %param.8) | data formatting | bytes 4194304 | tf_op args[0]
  30.7 1.5 broadcast.75
  32.2 25.2 %all-gather.3.cloned.1.call-done = bf16[2048,256]{1,0:T(8,128)(2,1)} async-done(((bf16[256,256]{1,0:T(8,128)(2,1)}), bf16[2048,256]{1,0:T(8,128)(2,1)}) %all-gather.3.cloned.1.call-update) | async-done | bytes 1048592 | tf_op jit(solution)/shard_map/all_gather | solution.py:61
  57.4 2.3 %copy.41 = bf16[2048,256]{0,1:T(8,128)(2,1)} copy(bf16[2048,256]{1,0:T(8,128)(2,1)} %all-gather.3.cloned.1.call-done) | data formatting | bytes 2097152 | tf_op jit(solution)/shard_map/all_gather | solution.py:61
  59.7 38.9 %all-gather.5.cloned.1.call-done = bf16[2048,256]{1,0:T(8,128)(2,1)} async-done(((bf16[256,256]{1,0:T(8,128)(2,1)}), bf16[2048,256]{1,0:T(8,128)(2,1)}) %all-gather.5.cloned.1.call-update) | async-done | bytes 1048592 | tf_op jit(solution)/shard_map/all_gather | solution.py:62
  98.6 2.3 %copy.43 = bf16[2048,256]{0,1:T(8,128)(2,1)} copy(bf16[2048,256]{1,0:T(8,128)(2,1)} %all-gather.5.cloned.1.call-done) | data formatting | bytes 2097152 | tf_op jit(solution)/shard_map/all_gather | solution.py:62
  100.8 49.0 %conditional.3 = (f32[256,2,8]{0,2,1:T(8,128)S(1)}, f32[256,2,8,128]{3,0,2,1:T(8,128)}) conditional(s32[]{:T(128)} %bitcast.20, (f32[256,2,8]{0,2,1:T(8,128)S(1)}, f32[256,2,8,128]{3,0,2,1:T(8,128)}) %tuple.33, (s32[2,256]{1,0:T(2,128)S(1)}, bf16[2,256,2,8,128]{1,4,3,2,0:T(8,128)(2,1)S(1)}, bf16[2048,2,128]{0,2,1:T(8,128)(2,1)}, ...), branch_computations={%region_4.0_spmd, %region_5.0_spmd} | conditional | flops 4388823040 | bytes 114527248 | solution.py:86
  100.8 0.3 iota_compare_fusion.1
  101.2 2.4 %copy.48 = bf16[2,256,2,8,128]{4,1,3,2,0:T(8,128)(2,1)} copy(bf16[2,256,2,8,128]{1,4,3,2,0:T(8,128)(2,1)S(1)} %get-tuple-element.189) | data formatting | bytes 4194304 | tf_op jit(solution)/shard_map
  103.6 15.0 %fusion.15 = (f32[256,2,8]{0,2,1:T(8,128)S(1)}, f32[2,2048,256,8]{2,1,3,0:T(8,128)}) fusion(pred[256,2048]{0,1:T(8,128)(4,1)S(1)} %iota_compare_fusion.1, bf16[2,256,2,8,128]{4,1,3,2,0:T(8,128)(2,1)} %copy.48, bf16[2048,2,128]{0,2,1:T(8,128)(2,1)} %get-tuple-element.190), kind=kOutput, calls=%fused_computation.21 | convolution fusion | flops 2172645376 | bytes 36192256 | tf_op jit(solution)/shard_map/while/body/eval_jaxpr/cond/branch_1_fun/rhgd,khd->rhgk/dot_general | solution.py:24
  118.5 14.4 %fusion.19 = f32[256,2,8]{0,2,1:T(8,128)S(1)} fusion(f32[2,2048,256,8]{2,1,3,0:T(8,128)} %get-tuple-element.202, f32[256,2,8]{0,2,1:T(8,128)S(1)} %max.7, pred[256,2048]{0,1:T(8,128)(4,1)S(1)} %iota_compare_fusion.1), kind=kLoop, calls=%fused_computation.25 | loop fusion | flops 33550336 | bytes 34111488 | tf_op jit(solution)/shard_map/while/body/eval_jaxpr/cond/branch_1_fun/reduce_sum | solution.py:32
  132.9 16.9 %bitcast_add_fusion.1 = f32[256,2,8,128]{3,0,2,1:T(8,128)} fusion(f32[256,2,8,128]{3,0,2,1:T(8,128)} %get-tuple-element.143, f32[2,2048,256,8]{2,1,3,0:T(8,128)} %get-tuple-element.202, f32[256,2,8]{0,2,1:T(8,128)S(1)} %max.7, pred[256,2048]{0,1:T(8,128)(4,1)S(1)} %iota_compare_fusion.1, bf16[2048,2,128]{0,2,1:T(8,128)(2,1)} %get-tuple-element.194, ...), kind=kOutput, calls=%fused_computation.28 | convolution fusion | flops 2182086656 | bytes 39354368 | tf_op jit(solution)/shard_map/while/body/eval_jaxpr/cond/branch_1_fun/rhgk,khd->rhgd/dot_general | solution.py:33
  149.8 1.9 divide_convert_fusion
  151.8 0.7 copy.51
  152.5 1.3 stack_reshape.7
  153.7 48.2 %conditional.2 = ((f32[256,2,8]{0,2,1:T(8,128)S(1)}, f32[256,2,8,128]{3,0,2,1:T(8,128)})) conditional(s32[]{:T(128)} %bitcast.12, (f32[256,2,8]{0,2,1:T(8,128)S(1)}, f32[256,2,8,128]{3,0,2,1:T(8,128)}) %tuple.33, (s32[2,256]{1,0:T(2,128)S(1)}, bf16[2,256,2,8,128]{1,4,3,2,0:T(8,128)(2,1)S(1)}, bf16[2048,2,128]{0,2,1:T(8,128)(2,1)}, ...), branch_computations={%region_0.1_spmd, %region_1.4_spmd} | conditional | flops 4388823040 | bytes 131304528 | solution.py:86
  153.7 0.3 iota_compare_fusion
  154.1 2.4 %copy.44 = bf16[2,256,2,8,128]{4,1,3,2,0:T(8,128)(2,1)} copy(bf16[2,256,2,8,128]{1,4,3,2,0:T(8,128)(2,1)S(1)} %get-tuple-element.182) | data formatting | bytes 4194304 | tf_op jit(solution)/shard_map
  156.5 15.0 %fusion = (f32[256,2,8]{0,2,1:T(8,128)S(1)}, f32[2,2048,256,8]{2,1,3,0:T(8,128)}) fusion(pred[256,2048]{0,1:T(8,128)(4,1)S(1)} %iota_compare_fusion, bf16[2,256,2,8,128]{4,1,3,2,0:T(8,128)(2,1)} %copy.44, bf16[2048,2,128]{0,2,1:T(8,128)(2,1)} %get-tuple-element.183), kind=kOutput, calls=%fused_computation.2 | convolution fusion | flops 2172645376 | bytes 36192256 | tf_op jit(solution)/shard_map/while/body/eval_jaxpr/cond/branch_1_fun/rhgd,khd->rhgk/dot_general | solution.py:24
  171.4 0.0 copy-start
  171.4 14.5 %fusion.4 = f32[256,2,8]{0,2,1:T(8,128)S(1)} fusion(f32[2,2048,256,8]{2,1,3,0:T(8,128)} %get-tuple-element.200, f32[256,2,8]{0,2,1:T(8,128)S(1)} %max.6, pred[256,2048]{0,1:T(8,128)(4,1)S(1)} %iota_compare_fusion), kind=kLoop, calls=%fused_computation.6 | loop fusion | flops 33550336 | bytes 34111488 | tf_op jit(solution)/shard_map/while/body/eval_jaxpr/cond/branch_1_fun/reduce_sum | solution.py:32
  186.0 0.0 copy-done
  186.0 14.6 %bitcast_add_fusion = f32[256,2,8,128]{3,0,2,1:T(8,128)S(1)} fusion(f32[256,2,8,128]{3,0,2,1:T(8,128)S(1)} %copy-done, f32[2,2048,256,8]{2,1,3,0:T(8,128)} %get-tuple-element.200, f32[256,2,8]{0,2,1:T(8,128)S(1)} %max.6, pred[256,2048]{0,1:T(8,128)(4,1)S(1)} %iota_compare_fusion, bf16[2048,2,128]{0,2,1:T(8,128)(2,1)} %get-tuple-element.187, ...), kind=kOutput, calls=%fused_computation.9 | convolution fusion | flops 2182086656 | bytes 39354368 | tf_op jit(solution)/shard_map/while/body/eval_jaxpr/cond/branch_1_fun/rhgk,khd->rhgd/dot_general | solution.py:33
  200.6 0.0 copy-start.1
  200.6 1.3 copy-done.1
  201.9 1.9 divide_convert_fusion.1
  203.9 0.7 copy.47
  204.6 0.5 stack_reshape.6
  205.1 2.7 %pad_maximum_fusion = bf16[2,256,2048]{2,1,0:T(8,128)(2,1)} fusion(bf16[1,256,2048]{2,1,0:T(8,128)(2,1)} %stack_reshape.7, bf16[1,256,2048]{2,1,0:T(8,128)(2,1)S(1)} %stack_reshape.6), kind=kLoop, calls=%fused_computation.38 | loop fusion | flops 1048576 | bytes 4194304 | tf_op jit(solution)/shard_map/stack | solution.py:95
  (8 shorter events, 0.0 us)
Async XLA Ops:
  6.5 50.9 %all-gather.3.cloned.1.call-start = ((), (), s32[]{:S(2)}) async-start(), calls=%async_computation.2 | async-start | bytes 1179648 | tf_op jit(solution)/shard_map/all_gather | solution.py:61
  16.2 82.3 %all-gather.5.cloned.1.call-start = ((), (), s32[]{:S(2)}) async-start(), calls=%async_computation.3 | async-start | bytes 1179648 | tf_op jit(solution)/shard_map/all_gather | solution.py:62
  171.4 14.5 %copy-start = (f32[256,2,8,128]{3,0,2,1:T(8,128)S(1)}, f32[256,2,8,128]{3,0,2,1:T(8,128)}, u32[]{:S(2)}) copy-start(f32[256,2,8,128]{3,0,2,1:T(8,128)} %get-tuple-element.136) | copy-start | bytes 6291460 | tf_op jit(solution)/shard_map/while/body/eval_jaxpr/cond
  200.6 1.3 copy-start.1
Sparse Core Ops, SparseCore 0:
  16.3 41.0 all-gather.2
  59.5 38.9 all-gather.4
where the time goes:
time: 215 us
  waiting for transfers between devices  64.1 us (30%)
  matrix products  61.4 us (29%)
  other arithmetic  37.1 us (17%)
  local copies, waits for them, and re-layouts  20.7 us (10%)
  blocking collectives  16.4 us (8%)
  between operations  14.8 us (7%)
    all_gather x1, waiting for transfers between devices, on_device(): value_piece = lax.all_gather(value_cols, 'pipe', axis=0, tiled=True)  38.9 us
    dot_general x2, matrix products, absorb(): jnp.einsum('rhgk,khd->rhgd', weights.astype(jnp.bfloat16), value_block, p...  31.5 us
    dot_general x2, matrix products, absorb(): jnp.einsum('rhgd,khd->rhgk', query, key_block, preferred_element_type=jnp...  29.9 us
    reduce_sum x2, other arithmetic, absorb(): total = total * factor + jnp.sum(weights, axis=-1)  28.8 us
    all_gather x1, waiting for transfers between devices, on_device(): key_piece = lax.all_gather(key_cols, 'pipe', axis=0, tiled=True)  25.2 us
    all_to_all x1, blocking collectives, on_device(): lax.all_to_all(keys, 'head', split_axis=1, concat_axis=0, tiled=True)  8.74 us
    all_to_all x1, blocking collectives, on_device(): lax.all_to_all(values, 'head', split_axis=1, concat_axis=0, tiled=True)  7.64 us
    another operation x5, local copies, waits for them, and re-layouts  6.32 us
  transfers between devices with their start and end apart: 2, of which 2 were waited for; matrix products, arithmetic and copies ran while one was open for 4% of the time, Pallas kernels for 0%

commit v1 on v0

v1 whole, which is shorter than its diff:
```python
import math

import jax
import jax.numpy as jnp
from jax import lax
from jax.experimental import pallas as pl
from jax.experimental.pallas import tpu as pltpu
from jax.sharding import PartitionSpec as P

HEAD_SIZE = 128
NEG = -1e30
TO_EXP2 = HEAD_SIZE ** (-0.5) * math.log2(math.e)
SUPER = 8
UNROLL = 2


def scores_of(query, key_block):
    return lax.dot_general(query, key_block, (((1,), (1,)), ((), ())), preferred_element_type=jnp.float32)


def weigh(scores, peak, value_block):
    weights = jnp.exp2((scores - peak) * TO_EXP2).astype(jnp.bfloat16)
    ones = jnp.ones(value_block.shape, jnp.bfloat16)
    return jnp.dot(weights, jnp.concatenate([value_block, ones], axis=1), preferred_element_type=jnp.float32)


def attend_kernel(slices, group, index_ref, q_ref, k_ref, v_ref, o_ref, best_ref, accum_ref):
    tick = pl.program_id(1)
    rows = q_ref.shape[1]
    mine = index_ref[tick]
    full = mine // SUPER
    rest = lax.rem(mine, SUPER) + 1
    several = slices > SUPER
    if several:
        best_ref[...] = jnp.full(best_ref.shape, NEG, jnp.float32)
        accum_ref[...] = jnp.zeros(accum_ref.shape, jnp.float32)

        @pl.loop(0, full)
        def _(step):
            at = pl.ds(pl.multiple_of(step * (SUPER * rows), SUPER * rows), SUPER * rows)

            @pl.loop(0, group)
            def _(g):
                query = q_ref[0, :, pl.ds(pl.multiple_of(g * HEAD_SIZE, HEAD_SIZE), HEAD_SIZE)]
                scores = scores_of(query, k_ref[at, :])
                before = best_ref[g]
                peak = jnp.maximum(before, jnp.max(scores, axis=-1, keepdims=True))
                best_ref[g] = peak
                accum_ref[g] = accum_ref[g] * jnp.exp2((before - peak) * TO_EXP2) + weigh(scores, peak, v_ref[at, :])

    low = lax.broadcasted_iota(jnp.int32, (rows, rows), 0) >= lax.broadcasted_iota(jnp.int32, (rows, rows), 1)
    for extent in range(1, min(SUPER, slices) + 1):

        @pl.when(rest == extent)
        def _(extent=extent):
            start = full * (SUPER * rows) if several else 0

            def one(g):
                columns = pl.ds(pl.multiple_of(g * HEAD_SIZE, HEAD_SIZE), HEAD_SIZE)
                query = q_ref[0, :, columns]
                at = pl.ds(pl.multiple_of(start, SUPER * rows), extent * rows) if several else pl.ds(0, extent * rows)
                scores = scores_of(query, k_ref[at, :])
                edge = jnp.where(low, scores[:, (extent - 1) * rows:], NEG)
                scores = jnp.concatenate([scores[:, :(extent - 1) * rows], edge], axis=1) if extent > 1 else edge
                peak = jnp.max(scores, axis=-1, keepdims=True)
                if several:
                    peak = jnp.maximum(peak, best_ref[g])
                result = weigh(scores, peak, v_ref[at, :])
                if several:
                    result = result + accum_ref[g] * jnp.exp2((best_ref[g] - peak) * TO_EXP2)
                o_ref[0, :, columns] = (result[:, :HEAD_SIZE] / result[:, HEAD_SIZE:]).astype(o_ref.dtype)

            @pl.loop(0, group // UNROLL)
            def _(step):
                for u in range(UNROLL):
                    one(step * UNROLL + u)


def attend(queries, key_all, value_all, index):
    ticks, rows, columns = queries.shape
    extent, width = key_all.shape
    heads = width // HEAD_SIZE
    group = columns // width
    slices = extent // rows
    state = group if slices > SUPER else 1
    return pl.pallas_call(
        lambda *refs: attend_kernel(slices, group, *refs),
        out_shape=jax.ShapeDtypeStruct(queries.shape, queries.dtype),
        grid_spec=pltpu.PrefetchScalarGridSpec(
            num_scalar_prefetch=1,
            grid=(heads, ticks),
            in_specs=[
                pl.BlockSpec((1, rows, group * HEAD_SIZE), lambda h, t, _: (t, 0, h)),
                pl.BlockSpec((extent, HEAD_SIZE), lambda h, t, _: (0, h)),
                pl.BlockSpec((extent, HEAD_SIZE), lambda h, t, _: (0, h)),
            ],
            out_specs=pl.BlockSpec((1, rows, group * HEAD_SIZE), lambda h, t, _: (t, 0, h)),
            scratch_shapes=[
                pltpu.VMEM((state, rows, 1), jnp.float32),
                pltpu.VMEM((state, rows, 2 * HEAD_SIZE), jnp.float32),
            ],
        ),
        compiler_params=pltpu.CompilerParams(vmem_limit_bytes=60 * 2 ** 20),
        name="attend",
    )(index, queries, key_all, value_all)


def on_device(queries, keys, values, slice_index):
    key_cols = lax.all_to_all(keys, "head", split_axis=1, concat_axis=0, tiled=True)
    value_cols = lax.all_to_all(values, "head", split_axis=1, concat_axis=0, tiled=True)
    key_all = lax.all_gather(key_cols, "pipe", axis=0, tiled=True)
    value_all = lax.all_gather(value_cols, "pipe", axis=0, tiled=True)
    index = lax.dynamic_index_in_dim(slice_index, lax.axis_index("pipe"), axis=1, keepdims=False)
    return attend(queries, key_all, value_all, index)


def solution(mesh):
    return jax.shard_map(
        on_device,
        mesh=mesh,
        in_specs=(
            P(None, "pipe", "head"),
            P(("pipe", "head"), None),
            P(("pipe", "head"), None),
            P(),
        ),
        out_specs=P(None, "pipe", "head"),
        check_vma=False,
    )
```

time: 215 us -> 134 us (0.62); the launches traced: 215 us -> 136 us
  matrix products: 61.4 us -> 0 us
  other arithmetic: 37.1 us -> 0 us
  Pallas kernels: 0 us -> 31 us
  local copies, waits for them, and re-layouts: 20.7 us -> 2.53 us
  waiting for transfers between devices: 64.1 us -> 73 us
    dot_general x4 -> x0, matrix products: 61.4 us -> none  [the longest x2 31.5 us: absorb(): jnp.einsum('rhgk,khd->rhgd', weights.astype(jnp.bfloat16), value_block, p...]
    pallas_call x0 -> x1, Pallas kernels: none -> 31 us  [attend(): pl.pallas_call(lambda *refs: attend_kernel(slices, group, *refs), out_sha...]
    reduce_sum x2 -> x0, other arithmetic: 28.8 us -> none  [absorb(): total = total * factor + jnp.sum(weights, axis=-1)]
    all_gather x2, waiting for transfers between devices: 64.1 us -> 72.9 us  [the longest x1 41.1 us: on_device(): value_all = lax.all_gather(value_cols, 'pipe', axis=0, tiled=True)]
    another operation x7 -> x0, local copies, waits for them, and re-layouts: 8.1 us -> none
    all_gather x2 -> x0, local copies, waits for them, and re-layouts: 4.54 us -> none  [the longest x1 2.27 us: on_device(): key_piece = lax.all_gather(key_cols, 'pipe', axis=0, tiled=True)]
    convert_element_type x2 -> x0, other arithmetic: 3.89 us -> none  [finish(): result = (accum / total[..., None]).astype(jnp.bfloat16)]
    unnamed x1 -> x2, local copies, waits for them, and re-layouts: 2.86 us -> 0.01 us
  transfers between devices with their start and end apart: 2 -> 2, of which waited for: 2 -> 2; matrix products, arithmetic and copies ran while one was open for 4% -> 1% of each run, Pallas kernels for 0% -> 0%
where the time goes in v1:
time: 134 us; the launch traced here: 136 us
  waiting for transfers between devices  73 us (54%)
  Pallas kernels  31 us (23%)
  blocking collectives  16.4 us (12%)
  between operations  13.4 us (10%)
  local copies, waits for them, and re-layouts  2.53 us (2%)
    all_gather x1, waiting for transfers between devices, on_device(): value_all = lax.all_gather(value_cols, 'pipe', axis=0, tiled=True)  41.1 us
    all_gather x1, waiting for transfers between devices, on_device(): key_all = lax.all_gather(key_cols, 'pipe', axis=0, tiled=True)  31.8 us
    pallas_call x1, Pallas kernels, attend(): pl.pallas_call(lambda *refs: attend_kernel(slices, group, *refs), out_sha...  31 us
    all_to_all x1, blocking collectives, on_device(): lax.all_to_all(keys, 'head', split_axis=1, concat_axis=0, tiled=True)  8.74 us
    all_to_all x1, blocking collectives, on_device(): lax.all_to_all(values, 'head', split_axis=1, concat_axis=0, tiled=True)  7.65 us
  transfers between devices with their start and end apart: 2, of which 2 were waited for; matrix products, arithmetic and copies ran while one was open for 1% of the time, Pallas kernels for 0%

profile of v1, /device:TPU:0, one launch (start us, length us, event | category | flops | bytes accessed | tf_op | source)
XLA Modules:
  0.0 136.4 jit_solution(3320537149072000236)
XLA Ops:
  6.5 0.0 copy-start
  6.5 0.0 all-gather.3.cloned.1.call-start
  6.5 0.9 copy.12
  7.5 8.7 %all_to_all.38 = bf16[64,4,256]{2,0,1:T(8,128)(2,1)} all-to-all(bf16[64,4,256]{2,0,1:T(8,128)(2,1)S(1)} %bitcast.16), channel_id=1, replica_groups=mesh['pipe'=8,'head'=4] {'head'}, dimensions={1} | all-to-all | bytes 262144 | tf_op jit(solution)/shard_map/all_to_all | solution.py:109
  16.2 0.0 all-gather.3.cloned.1.call-update
  16.2 0.0 all-gather.5.cloned.1.call-start
  16.3 0.9 copy.11
  17.2 7.7 %all_to_all.39 = bf16[64,4,256]{2,0,1:T(8,128)(2,1)} all-to-all(bf16[64,4,256]{2,0,1:T(8,128)(2,1)S(1)} %bitcast.17), channel_id=1, replica_groups=mesh['pipe'=8,'head'=4] {'head'}, dimensions={1} | all-to-all | bytes 262144 | tf_op jit(solution)/shard_map/all_to_all | solution.py:110
  24.9 0.0 all-gather.5.cloned.1.call-update
  24.9 0.0 copy-done
  24.9 0.7 dynamic-slice_reduce_fusion.refs_0_
  25.6 31.8 %all-gather.3.cloned.1.call-done.refs_2_ = bf16[2048,256]{1,0:T(8,128)(2,1)} async-done(((bf16[256,256]{1,0:T(8,128)(2,1)}), bf16[2048,256]{1,0:T(8,128)(2,1)}) %all-gather.3.cloned.1.call-update) | async-done | bytes 1048592 | tf_op jit(solution)/shard_map/all_gather | solution.py:111
  57.4 41.1 %all-gather.5.cloned.1.call-done.refs_3_ = bf16[2048,256]{1,0:T(8,128)(2,1)} async-done(((bf16[256,256]{1,0:T(8,128)(2,1)}), bf16[2048,256]{1,0:T(8,128)(2,1)}) %all-gather.5.cloned.1.call-update) | async-done | bytes 1048592 | tf_op jit(solution)/shard_map/all_gather | solution.py:112
  98.5 31.0 %attend.1 = bf16[2,256,2048]{2,1,0:T(8,128)(2,1)} custom-call(s32[2]{0:T(128)} %dynamic-slice_reduce_fusion.refs_0_, bf16[2,256,2048]{2,1,0:T(8,128)(2,1)} %refs_1_.1, bf16[2048,256]{1,0:T(8,128)(2,1)} %all-gather.3.cloned.1.call-done.refs_2_, bf16[2048,256]{1,0:T(8,128)(2,1)} %all-gather.5.cloned.1.call-done.refs_3_), custom_call_target="tpu_custom_call" | custom-call | tf_op jit(solution)/shard_map/attend/pallas_call | solution.py:86
Async XLA Ops:
  6.5 18.4 %copy-start = (s32[2,8]{1,0:T(2,128)S(1)}, s32[2,8]{1,0:T(2,128)}, u32[]{:S(2)}) copy-start(s32[2,8]{1,0:T(2,128)} %param.7) | copy-start | bytes 196
  6.5 50.8 %all-gather.3.cloned.1.call-start = ((), (), s32[]{:S(2)}) async-start(), calls=%async_computation.2 | async-start | bytes 1179648 | tf_op jit(solution)/shard_map/all_gather | solution.py:111
  16.2 82.3 %all-gather.5.cloned.1.call-start = ((), (), s32[]{:S(2)}) async-start(), calls=%async_computation.3 | async-start | bytes 1179648 | tf_op jit(solution)/shard_map/all_gather | solution.py:112
Sparse Core Ops, SparseCore 0:
  16.4 40.9 all-gather.2
  59.5 38.9 all-gather.4
